TPU v7x, 128 devices: a whole 4x4x4 slice. The times are simulated.
128 devices in a mesh: row: 8 (over z, x_hi), col: 16 (over y, x_lo, core).
Axes of the slice: x: 4 (x_hi: 2, x_lo: 2; x = x_hi * 2 + x_lo), y: 4, z: 4, core: 2. Of those that a mesh axis runs over, the one named last changes fastest.
Arguments:
- features: bfloat16 [32768, 512], P('row'), may hold values from -6 to 6
- logits: float32 [32768, 128], P(('row', 'col')), may hold values from -16 to 16
Outputs:
- memberships: float32 [32768, 128], P(('row', 'col'))
- standardized: float32 [32768, 128], P(('row', 'col'))
All inputs are finite; a program needn't handle non-finite values.
Results may differ from a plain program's by a relative error of at most 0.0003.
Values may be sent and summed in bfloat16 or wider, within the bound.
A program may use at most 64 MiB of HBM per device.

v0:
```python
import math
import jax
import jax.numpy as jnp
from jax import lax
from jax.sharding import PartitionSpec as P

ITERS = 2


def kernel_product(left_rows, right_rows, members):
    count = left_rows.shape[0]
    feature_width = left_rows.shape[1]
    block_rows = math.gcd(count, 512)
    blocks = left_rows.reshape(count // block_rows, block_rows, feature_width)

    def block_product(block):
        inner = jnp.einsum("bf,nf->bn", block, right_rows, preferred_element_type=jnp.float32)
        base = 1.0 + inner / feature_width
        kernel = base * base * base
        return jnp.dot(
            kernel, members, precision=lax.Precision.HIGHEST, preferred_element_type=jnp.float32
        )

    return lax.map(block_product, blocks).reshape(count, members.shape[1])


def on_device(features, logits):
    frames = logits.shape[0]
    column = lax.axis_index("col")
    own_rows = lax.dynamic_slice_in_dim(features, column * frames, frames, 0)
    column_panel = lax.all_gather(own_rows, "row", axis=0, tiled=True)
    raised = jnp.exp(logits)
    members = raised / jnp.sum(raised, axis=1, keepdims=True)
    standardized = members
    for iteration in range(ITERS):
        members_column = lax.all_gather(members, "row", axis=0, tiled=True)
        scores = lax.psum_scatter(
            kernel_product(features, column_panel, members_column),
            "col",
            scatter_dimension=0,
            tiled=True,
        )
        cluster_size, weighted = lax.psum(
            (jnp.sum(members, axis=0), jnp.sum(members * scores, axis=0)), ("row", "col")
        )
        compact = weighted / (cluster_size * cluster_size)
        distance = compact[None, :] - 2.0 * scores / cluster_size[None, :]
        centered = distance - jnp.mean(distance, axis=1, keepdims=True)
        spread = jnp.mean(centered * centered, axis=1, keepdims=True)
        standardized = centered / jnp.sqrt(spread + 1e-06)
        raised = jnp.exp(-2.0 * standardized)
        members = raised / jnp.sum(raised, axis=1, keepdims=True)
    return (members, standardized)


def solution(mesh):
    return jax.shard_map(
        on_device,
        mesh=mesh,
        in_specs=(P("row", None), P(("row", "col"), None)),
        out_specs=(P(("row", "col"), None), P(("row", "col"), None)),
        check_vma=False,
    )
```

profile of v0, /device:TPU:1, one launch (start us, length us, event | category | flops | bytes accessed | tf_op | source)
XLA Modules:
  0.0 545.2 jit_solution(2299477837792060629)
XLA Ops:
  11.7 47.2 %all-gather.6.cloned.1.call-done = f32[2048,128]{1,0:T(8,128)} async-done(((f32[256,128]{1,0:T(8,128)}), f32[2048,128]{1,0:T(8,128)}) %all-gather.6.cloned.1.call-update) | async-done | bytes 1048592 | tf_op jit(solution)/shard_map/all_gather | solution.py:36
  59.0 55.7 %all-gather.4.cloned.1.call-done = bf16[2048,512]{1,0:T(8,128)(2,1)} async-done(((bf16[256,512]{1,0:T(8,128)(2,1)}), bf16[2048,512]{1,0:T(8,128)(2,1)}) %all-gather.4.cloned.1.call-update) | async-done | bytes 2097168 | tf_op jit(solution)/shard_map/all_gather | solution.py:31
  114.8 54.8 %while.20 = (s32[]{:T(128)}, f32[8,512,128]{2,1,0:T(8,128)S(1)}, bf16[8,512,512]{2,1,0:T(8,128)(2,1)}, bf16[2048,512]{1,0:T(8,128)(2,1)}, f32[2048,128]{1,0:T(8,128)}, /*index=5*/s32[]{:T(128)}) while((s32[]{:T(128)}, f32[8,512,128]{2,1,0:T(8,128)S(1)}, bf16[8,512,512]{2,1,0:T(8,128)(2,1)}, bf16[2048,512]{1,0:T(8,128)(2,1)}, ...), condition=%wide.region_2.3_spmd, body=%wide.region_1.2_spmd.sunk | while | flops 2688548864 | bytes 16515685 | solution.py:24
  118.0 3.7 fusion.49
  124.9 3.7 fusion.49
  131.7 3.7 fusion.49
  138.6 3.7 fusion.49
  145.4 3.7 fusion.49
  152.3 3.7 fusion.49
  159.1 3.7 fusion.49
  166.0 3.7 fusion.49
  171.0 60.5 %reduce-scatter.3.cloned.1.call-done = f32[256,128]{1,0:T(8,128)} async-done(((f32[4096,128]{1,0:T(8,128)}), f32[256,128]{1,0:T(8,128)}) %reduce-scatter.3.cloned.1.call-update) | async-done | bytes 131088 | tf_op jit(solution)/shard_map/reduce_scatter | solution.py:37
  232.5 68.0 %all-reduce.1 = (f32[128]{0:T(128)S(1)}, f32[128]{0:T(128)S(1)}) all-reduce(f32[128]{0:T(128)S(1)} %get-tuple-element.61, f32[128]{0:T(128)S(1)} %get-tuple-element.60), channel_id=1, replica_groups=mesh['row'=8,'col'=16] {'row','col'}, use_global_device_ids=true, to_apply=%region_7.8 | all-reduce | flops 256 | bytes 2048 | tf_op jit(solution)/shard_map/psum | solution.py:43
  305.8 41.2 %all-gather.8.cloned.1.call-done = f32[2048,128]{1,0:T(8,128)} async-done(((f32[256,128]{1,0:T(8,128)}), f32[2048,128]{1,0:T(8,128)}) %all-gather.8.cloned.1.call-update) | async-done | bytes 1048592 | tf_op jit(solution)/shard_map/all_gather | solution.py:36
  347.2 54.8 %while.21 = (s32[]{:T(128)}, f32[8,512,128]{2,1,0:T(8,128)S(1)}, bf16[8,512,512]{2,1,0:T(8,128)(2,1)}, bf16[2048,512]{1,0:T(8,128)(2,1)}, f32[2048,128]{1,0:T(8,128)}, /*index=5*/s32[]{:T(128)}) while((s32[]{:T(128)}, f32[8,512,128]{2,1,0:T(8,128)S(1)}, bf16[8,512,512]{2,1,0:T(8,128)(2,1)}, bf16[2048,512]{1,0:T(8,128)(2,1)}, ...), condition=%wide.region_12.13_spmd, body=%wide.region_11.12_spmd.sunk | while | flops 2688548864 | bytes 16515685 | solution.py:24
  350.3 3.7 fusion.54
  357.2 3.7 fusion.54
  364.1 3.7 fusion.54
  370.9 3.7 fusion.54
  377.8 3.7 fusion.54
  384.6 3.7 fusion.54
  391.5 3.7 fusion.54
  403.4 62.6 %reduce-scatter.5.cloned.1.call-done = f32[256,128]{1,0:T(8,128)} async-done(((f32[4096,128]{1,0:T(8,128)}), f32[256,128]{1,0:T(8,128)}) %reduce-scatter.5.cloned.1.call-update) | async-done | bytes 131088 | tf_op jit(solution)/shard_map/reduce_scatter | solution.py:37
  467.1 67.5 %all-reduce = (f32[128]{0:T(128)S(1)}, f32[128]{0:T(128)S(1)}) all-reduce(f32[128]{0:T(128)S(1)} %get-tuple-element.59, f32[128]{0:T(128)S(1)} %get-tuple-element.58), channel_id=1, replica_groups=mesh['row'=8,'col'=16] {'row','col'}, use_global_device_ids=true, to_apply=%region_17.18 | all-reduce | flops 256 | bytes 2048 | tf_op jit(solution)/shard_map/psum | solution.py:43
  (90 shorter events, 72.6 us)
Async XLA Ops:
  7.2 51.8 %all-gather.6.cloned.1.call-start = ((), (), s32[]{:S(2)}) async-start(), calls=%async_computation.3 | async-start | bytes 1179648 | tf_op jit(solution)/shard_map/all_gather | solution.py:36
  9.9 104.8 %all-gather.4.cloned.1.call-start = ((), (), s32[]{:S(2)}) async-start(), calls=%async_computation.2 | async-start | bytes 2359296 | tf_op jit(solution)/shard_map/all_gather | solution.py:31
  11.7 219.8 %reduce-scatter.3.cloned.1.call-start = ((), (), s32[]{:S(2)}) async-start(), calls=%async_computation.4 | async-start | bytes 2228224 | tf_op jit(solution)/shard_map/reduce_scatter | solution.py:37
  114.8 116.7 %copy-start.3 = (f32[256,128]{1,0:T(8,128)S(1)}, f32[256,128]{1,0:T(8,128)}, u32[]{:S(2)}) copy-start(f32[256,128]{1,0:T(8,128)} %param.7) | copy-start | bytes 393220
  114.8 3.1 copy-start.5
  121.7 3.1 copy-start.5
  128.6 3.1 copy-start.5
  135.4 3.1 copy-start.5
  142.3 3.1 copy-start.5
  149.1 3.1 copy-start.5
  156.0 3.1 copy-start.5
  162.8 3.1 copy-start.5
  171.0 176.0 %all-gather.8.cloned.1.call-start = ((), (), s32[]{:S(2)}) async-start(), calls=%async_computation.5 | async-start | bytes 1179648 | tf_op jit(solution)/shard_map/all_gather | solution.py:36
  305.6 160.4 %reduce-scatter.5.cloned.1.call-start = ((), (), s32[]{:S(2)}) async-start(), calls=%async_computation.6 | async-start | bytes 2228224 | tf_op jit(solution)/shard_map/reduce_scatter | solution.py:37
  347.2 118.8 %copy-start.2 = (f32[256,128]{1,0:T(8,128)S(1)}, f32[256,128]{1,0:T(8,128)}, u32[]{:S(2)}) copy-start(f32[256,128]{1,0:T(8,128)} %reduce-scatter.3.cloned.1.call-done) | copy-start | bytes 393220
  347.2 3.1 copy-start.6
  354.1 3.1 copy-start.6
  360.9 3.1 copy-start.6
  367.8 3.1 copy-start.6
  374.6 3.1 copy-start.6
  381.5 3.1 copy-start.6
  388.3 3.1 copy-start.6
  395.2 3.1 copy-start.6
  402.0 1.4 copy-start
  (2 other events, 2.1 us)
Sparse Core Ops, SparseCore 0:
  10.9 48.0 all-gather.5
  61.3 53.3 all-gather.3
  171.1 60.3 reduce-scatter.2
  305.7 41.2 all-gather.7
  403.5 62.4 reduce-scatter.4
where the time goes:
time: 546 us; the launch traced here: 545 us
  waiting for transfers between devices  267 us (49%)
  blocking collectives  136 us (25%)
  matrix products  109 us (20%)
  between operations  13.9 us (3%)
  other arithmetic  13.8 us (3%)
    psum x2, blocking collectives, on_device(): lax.psum((jnp.sum(members, axis=0), jnp.sum(members * scores, axis=0)), (...  136 us
    reduce_scatter x2, waiting for transfers between devices, on_device(): lax.psum_scatter(kernel_product(features, column_panel, members_column),...  123 us
    all_gather x2, waiting for transfers between devices, on_device(): members_column = lax.all_gather(members, 'row', axis=0, tiled=True)  88.4 us
    dot_general x16, matrix products, block_product(): jnp.dot(kernel, members, precision=lax.Precision.HIGHEST, preferred_eleme...  58.9 us
    all_gather x1, waiting for transfers between devices, on_device(): column_panel = lax.all_gather(own_rows, 'row', axis=0, tiled=True)  55.7 us
    dot_general x16, matrix products, block_product(): jnp.einsum('bf,nf->bn', block, right_rows, preferred_element_type=jnp.flo...  50 us
  transfers between devices with their start and end apart: 5, of which 5 were waited for; matrix products, arithmetic and copies ran while one was open for 0% of the time, Pallas kernels for 0%

commit v1 on v0

--- a/solution.py
+++ b/solution.py
@@ -41,7 +41,7 @@
             tiled=True,
         )
         cluster_size, weighted = lax.psum(
-            (jnp.sum(members, axis=0), jnp.sum(members * scores, axis=0)), ("row", "col")
+            lax.psum((jnp.sum(members, axis=0), jnp.sum(members * scores, axis=0)), "col"), "row"
         )
         compact = weighted / (cluster_size * cluster_size)
         distance = compact[None, :] - 2.0 * scores / cluster_size[None, :]

time: 546 us -> 517 us (0.947)
  blocking collectives: 136 us -> 102 us
    psum x2 -> x4, blocking collectives: 136 us -> 102 us  [the longest x2 60.9 us: on_device(): lax.psum((jnp.sum(members, axis=0), jnp.sum(members * scores, axis=0)), '...]
where the time goes in v1:
time: 517 us; the launch traced here: 513 us
  waiting for transfers between devices  269 us (52%)
  matrix products  109 us (21%)
  blocking collectives  102 us (20%)
  between operations  13.9 us (3%)
  other arithmetic  13.8 us (3%)
    reduce_scatter x2, waiting for transfers between devices, on_device(): lax.psum_scatter(kernel_product(features, column_panel, members_column),...  123 us
    all_gather x2, waiting for transfers between devices, on_device(): members_column = lax.all_gather(members, 'row', axis=0, tiled=True)  90.4 us
    psum x2, blocking collectives, on_device(): lax.psum((jnp.sum(members, axis=0), jnp.sum(members * scores, axis=0)), '...  60.9 us
    dot_general x16, matrix products, block_product(): jnp.dot(kernel, members, precision=lax.Precision.HIGHEST, preferred_eleme...  58.9 us
    all_gather x1, waiting for transfers between devices, on_device(): column_panel = lax.all_gather(own_rows, 'row', axis=0, tiled=True)  55.7 us
    dot_general x16, matrix products, block_product(): jnp.einsum('bf,nf->bn', block, right_rows, preferred_element_type=jnp.flo...  50 us
    psum x2, blocking collectives, on_device(): lax.psum(lax.psum((jnp.sum(members, axis=0), jnp.sum(members * scores, ax...  40.8 us
  transfers between devices with their start and end apart: 5, of which 5 were waited for; matrix products, arithmetic and copies ran while one was open for 0% of the time, Pallas kernels for 0%

profile of v1, /device:TPU:1, one launch (start us, length us, event | category | flops | bytes accessed | tf_op | source)
XLA Modules:
  0.0 513.0 jit_solution(9180798623922746307)
XLA Ops:
  11.7 47.2 %all-gather.6.cloned.1.call-done = f32[2048,128]{1,0:T(8,128)} async-done(((f32[256,128]{1,0:T(8,128)}), f32[2048,128]{1,0:T(8,128)}) %all-gather.6.cloned.1.call-update) | async-done | bytes 1048592 | tf_op jit(solution)/shard_map/all_gather | solution.py:36
  59.0 55.7 %all-gather.4.cloned.1.call-done = bf16[2048,512]{1,0:T(8,128)(2,1)} async-done(((bf16[256,512]{1,0:T(8,128)(2,1)}), bf16[2048,512]{1,0:T(8,128)(2,1)}) %all-gather.4.cloned.1.call-update) | async-done | bytes 2097168 | tf_op jit(solution)/shard_map/all_gather | solution.py:31
  114.8 54.8 %while.20 = (s32[]{:T(128)}, f32[8,512,128]{2,1,0:T(8,128)S(1)}, bf16[8,512,512]{2,1,0:T(8,128)(2,1)}, bf16[2048,512]{1,0:T(8,128)(2,1)}, f32[2048,128]{1,0:T(8,128)}, /*index=5*/s32[]{:T(128)}) while((s32[]{:T(128)}, f32[8,512,128]{2,1,0:T(8,128)S(1)}, bf16[8,512,512]{2,1,0:T(8,128)(2,1)}, bf16[2048,512]{1,0:T(8,128)(2,1)}, ...), condition=%wide.region_2.3_spmd, body=%wide.region_1.2_spmd.sunk | while | flops 2688548864 | bytes 16515685 | solution.py:24
  118.0 3.7 fusion.49
  124.9 3.7 fusion.49
  131.7 3.7 fusion.49
  145.4 3.7 fusion.49
  152.3 3.7 fusion.49
  159.1 3.7 fusion.49
  166.0 3.7 fusion.49
  171.0 60.5 %reduce-scatter.3.cloned.1.call-done = f32[256,128]{1,0:T(8,128)} async-done(((f32[4096,128]{1,0:T(8,128)}), f32[256,128]{1,0:T(8,128)}) %reduce-scatter.3.cloned.1.call-update) | async-done | bytes 131088 | tf_op jit(solution)/shard_map/reduce_scatter | solution.py:37
  232.6 30.5 %all-reduce.1 = (f32[128]{0:T(128)S(1)}, f32[128]{0:T(128)S(1)}) all-reduce(f32[128]{0:T(128)S(1)} %get-tuple-element.61, f32[128]{0:T(128)S(1)} %get-tuple-element.60), channel_id=1, replica_groups=mesh['row'=8,'col'=16] {'col'}, use_global_device_ids=true, to_apply=%region_8.9 | all-reduce | flops 256 | bytes 2048 | tf_op jit(solution)/shard_map/psum | solution.py:44
  263.0 20.3 %all-reduce.3 = (f32[128]{0:T(128)S(1)}, f32[128]{0:T(128)S(1)}) all-reduce(f32[128]{0:T(128)S(1)} %get-tuple-element.84, f32[128]{0:T(128)S(1)} %get-tuple-element.85), channel_id=1, replica_groups=mesh['row'=8,'col'=16] {'row'}, use_global_device_ids=true, to_apply=%region_9.10 | all-reduce | flops 256 | bytes 2048 | tf_op jit(solution)/shard_map/psum | solution.py:43
  288.5 43.2 %all-gather.8.cloned.1.call-done = f32[2048,128]{1,0:T(8,128)} async-done(((f32[256,128]{1,0:T(8,128)}), f32[2048,128]{1,0:T(8,128)}) %all-gather.8.cloned.1.call-update) | async-done | bytes 1048592 | tf_op jit(solution)/shard_map/all_gather | solution.py:36
  331.8 54.8 %while.21 = (s32[]{:T(128)}, f32[8,512,128]{2,1,0:T(8,128)S(1)}, bf16[8,512,512]{2,1,0:T(8,128)(2,1)}, bf16[2048,512]{1,0:T(8,128)(2,1)}, f32[2048,128]{1,0:T(8,128)}, /*index=5*/s32[]{:T(128)}) while((s32[]{:T(128)}, f32[8,512,128]{2,1,0:T(8,128)S(1)}, bf16[8,512,512]{2,1,0:T(8,128)(2,1)}, bf16[2048,512]{1,0:T(8,128)(2,1)}, ...), condition=%wide.region_14.15_spmd, body=%wide.region_13.14_spmd.sunk | while | flops 2688548864 | bytes 16515685 | solution.py:24
  335.0 3.7 fusion.54
  341.8 3.7 fusion.54
  348.7 3.7 fusion.54
  362.4 3.7 fusion.54
  369.3 3.7 fusion.54
  376.1 3.7 fusion.54
  388.0 62.5 %reduce-scatter.5.cloned.1.call-done = f32[256,128]{1,0:T(8,128)} async-done(((f32[4096,128]{1,0:T(8,128)}), f32[256,128]{1,0:T(8,128)}) %reduce-scatter.5.cloned.1.call-update) | async-done | bytes 131088 | tf_op jit(solution)/shard_map/reduce_scatter | solution.py:37
  451.6 30.4 %all-reduce = (f32[128]{0:T(128)S(1)}, f32[128]{0:T(128)S(1)}) all-reduce(f32[128]{0:T(128)S(1)} %get-tuple-element.59, f32[128]{0:T(128)S(1)} %get-tuple-element.58), channel_id=1, replica_groups=mesh['row'=8,'col'=16] {'col'}, use_global_device_ids=true, to_apply=%region_20.21 | all-reduce | flops 256 | bytes 2048 | tf_op jit(solution)/shard_map/psum | solution.py:44
  482.0 20.4 %all-reduce.2 = (f32[128]{0:T(128)S(1)}, f32[128]{0:T(128)S(1)}) all-reduce(f32[128]{0:T(128)S(1)} %get-tuple-element.82, f32[128]{0:T(128)S(1)} %get-tuple-element.83), channel_id=1, replica_groups=mesh['row'=8,'col'=16] {'row'}, use_global_device_ids=true, to_apply=%region_21.22 | all-reduce | flops 256 | bytes 2048 | tf_op jit(solution)/shard_map/psum | solution.py:43
  (92 shorter events, 79.8 us)
Async XLA Ops:
  7.2 51.8 %all-gather.6.cloned.1.call-start = ((), (), s32[]{:S(2)}) async-start(), calls=%async_computation.3 | async-start | bytes 1179648 | tf_op jit(solution)/shard_map/all_gather | solution.py:36
  9.9 104.8 %all-gather.4.cloned.1.call-start = ((), (), s32[]{:S(2)}) async-start(), calls=%async_computation.2 | async-start | bytes 2359296 | tf_op jit(solution)/shard_map/all_gather | solution.py:31
  11.7 219.8 %reduce-scatter.3.cloned.1.call-start = ((), (), s32[]{:S(2)}) async-start(), calls=%async_computation.4 | async-start | bytes 2228224 | tf_op jit(solution)/shard_map/reduce_scatter | solution.py:37
  114.8 116.7 %copy-start.3 = (f32[256,128]{1,0:T(8,128)S(1)}, f32[256,128]{1,0:T(8,128)}, u32[]{:S(2)}) copy-start(f32[256,128]{1,0:T(8,128)} %param.7) | copy-start | bytes 393220
  114.8 3.1 copy-start.5
  121.7 3.1 copy-start.5
  128.6 3.1 copy-start.5
  135.4 3.1 copy-start.5
  142.3 3.1 copy-start.5
  149.1 3.1 copy-start.5
  156.0 3.1 copy-start.5
  162.8 3.1 copy-start.5
  171.0 160.7 %all-gather.8.cloned.1.call-start = ((), (), s32[]{:S(2)}) async-start(), calls=%async_computation.5 | async-start | bytes 1179648 | tf_op jit(solution)/shard_map/all_gather | solution.py:36
  288.4 162.1 %reduce-scatter.5.cloned.1.call-start = ((), (), s32[]{:S(2)}) async-start(), calls=%async_computation.6 | async-start | bytes 2228224 | tf_op jit(solution)/shard_map/reduce_scatter | solution.py:37
  331.8 118.7 %copy-start.2 = (f32[256,128]{1,0:T(8,128)S(1)}, f32[256,128]{1,0:T(8,128)}, u32[]{:S(2)}) copy-start(f32[256,128]{1,0:T(8,128)} %reduce-scatter.3.cloned.1.call-done) | copy-start | bytes 393220
  331.8 3.1 copy-start.6
  338.7 3.1 copy-start.6
  345.6 3.1 copy-start.6
  352.4 3.1 copy-start.6
  359.3 3.1 copy-start.6
  366.1 3.1 copy-start.6
  373.0 3.1 copy-start.6
  379.8 3.1 copy-start.6
  386.7 1.4 copy-start
  (2 other events, 2.1 us)
Sparse Core Ops, SparseCore 0:
  10.9 48.0 all-gather.5
  61.3 53.3 all-gather.3
  171.1 60.3 reduce-scatter.2
  288.5 43.0 all-gather.7
  388.2 62.3 reduce-scatter.4
